TPU v7x, 32 devices: a whole 2x2x4 slice. The times are simulated.
32 devices in a mesh: shot: 2 (over y), box: 8 (over z, x), sub: 2 (over core).
Axes of the slice: x: 2, y: 2, z: 4, core: 2. Of those that a mesh axis runs over, the one named last changes fastest.
Arguments:
- box_weights: float32 [64, 256, 128], P(('shot', 'box', 'sub')), parts along dimension 0, may hold values from -6 to 6
- velocity: float32 [8192], P('shot'), parts along dimension 0, may hold values from -4 to 4
- switch_kernel: float32 [128, 128], replicated, may hold values from -0.5 to 0.5
Outputs:
- final_weights: float32 [4, 4096, 128], P('shot', ('box', 'sub')), parts along dimension 0
There are 2 independent parts, one for each index of `shot`. A program takes and returns all parts, laid end to end along the dimension named above; an argument that names none is the same for every part. Nothing has to cross between parts.
All inputs are finite; a program needn't handle non-finite values.
Results may differ from a plain program's by a relative error of at most 0.00013.
Values sent between devices are 32-bit elements; how exact they have to be, the bound alone decides.
No kernel may reach another device: no remote copies, remote signals or barrier semaphores. Data moves between devices by JAX's collectives and lax.ppermute only.
A program may use at most 64 MiB of HBM per device.

v0:
```python
import jax
import jax.numpy as jnp
from jax import lax
from jax.sharding import PartitionSpec as P

CHEB = 8
half_root = 0.7071067811865476


def swapped(value, axis, apart):
    mask = 2**apart
    pairs = [(source, source ^ mask) for source in range(lax.axis_size(axis))]
    return lax.ppermute(value, axis, pairs)


def cheb_nodes():
    counter = jnp.arange(CHEB, dtype=jnp.float32)
    return jnp.cos(jnp.pi * (2.0 * counter + 1.0) / (2.0 * CHEB))


def lagrange_rows(points, node_values):
    differences = points[:, None] - node_values[None, :]
    node_gaps = node_values[:, None] - node_values[None, :]
    identity = jnp.eye(CHEB, dtype=jnp.float32)
    numerator = jnp.prod(
        jnp.where(identity[None, :, :] > 0.5, 1.0, differences[:, None, :]), axis=2
    )
    denominator = jnp.prod(jnp.where(identity > 0.5, 1.0, node_gaps), axis=1)
    return numerator / denominator[None, :]


def spread_coord(values, axis_dim):
    if axis_dim == 0:
        return jnp.repeat(values, CHEB)
    return jnp.tile(values, CHEB)


def level_tables(axis_dim):
    node_values = cheb_nodes()
    identity = jnp.eye(CHEB, dtype=jnp.float32)
    pair_eye = jnp.eye(2, dtype=jnp.float32)
    matrices = []
    coords = []
    for child_idx in (0, 1):
        child_pts = (node_values + (2.0 * child_idx - 1.0)) * 0.5
        lagrange = lagrange_rows(child_pts, node_values)
        if axis_dim == 0:
            single = jnp.kron(lagrange, identity)
        else:
            single = jnp.kron(identity, lagrange)
        matrices.append(jnp.kron(pair_eye, single))
        coords.append(spread_coord(child_pts, axis_dim))
    return (jnp.concatenate(matrices, 0), jnp.stack(coords), spread_coord(node_values, axis_dim))


def rotate(values, angles):
    real_part = values[..., : CHEB * CHEB]
    imag_part = values[..., CHEB * CHEB :]
    cosines = jnp.cos(angles)
    sine_vals = jnp.sin(angles)
    return jnp.concatenate(
        [real_part * cosines - imag_part * sine_vals, real_part * sine_vals + imag_part * cosines],
        -1,
    )


def merge_blocks(blocks, omegas, weights, coord_in, coord_out):
    phase = omegas[None, None, :, :, None]
    first_term = rotate(blocks[:, 0][:, :, None], -phase * coord_in[0])
    second_term = rotate(blocks[:, 1][:, :, None], -phase * coord_in[1])
    joined = jnp.concatenate([first_term, second_term], -1)
    mixture = jnp.dot(
        joined.reshape(-1, 4 * CHEB * CHEB),
        weights,
        precision=lax.Precision.HIGHEST,
        preferred_element_type=jnp.float32,
    )
    mixture = mixture.reshape(first_term.shape)
    return rotate(mixture, phase * coord_out) * half_root


def apply_switch(current, switch_kernel):
    flat = jnp.dot(
        current.reshape(-1, current.shape[-1]),
        switch_kernel,
        precision=lax.Precision.HIGHEST,
        preferred_element_type=jnp.float32,
    )
    return flat.reshape(current.shape)


def level_omegas(velocity, device, level_idx, tgt_count):
    tgt_code = device % 2 ** (level_idx + 1)
    return lax.dynamic_slice_in_dim(velocity, tgt_code * tgt_count, tgt_count)


def own_part(current, omegas, my_child, level_idx):
    vec_len = current.shape[-1]
    weights, coord_in, coord_out = level_tables(level_idx % 2)
    coord_mine = jnp.where(my_child == 0, coord_in[0], coord_in[1])
    weight_mine = jnp.where(my_child == 0, weights[:vec_len], weights[vec_len:])
    turned = rotate(current, -omegas[None, :, None] * coord_mine[None, None, :])
    return jnp.dot(
        turned.reshape(-1, vec_len),
        weight_mine,
        precision=lax.Precision.HIGHEST,
        preferred_element_type=jnp.float32,
    )


def far_part(own_term, partner, omegas, my_child, level_idx):
    vec_len = partner.shape[-1]
    weights, coord_in, coord_out = level_tables(level_idx % 2)
    coord_other = jnp.where(my_child == 0, coord_in[1], coord_in[0])
    weight_other = jnp.where(my_child == 0, weights[vec_len:], weights[:vec_len])
    turned = rotate(partner, -omegas[None, :, None] * coord_other[None, None, :])
    far_term = jnp.dot(
        turned.reshape(-1, vec_len),
        weight_other,
        precision=lax.Precision.HIGHEST,
        preferred_element_type=jnp.float32,
    )
    mixture = (own_term + far_term).reshape(partner.shape)
    return rotate(mixture, omegas[None, :, None] * coord_out[None, None, :]) * half_root


def body(box_weights, velocity, switch_kernel):
    box_count = lax.axis_size("box")
    sub_count = lax.axis_size("sub")
    box_bits = box_count.bit_length() - 1
    sub_bits = sub_count.bit_length() - 1
    levels = box_bits + sub_bits
    box_index = lax.axis_index("box")
    sub_index = lax.axis_index("sub")
    device = box_index * sub_count + sub_index
    src_count = box_weights.shape[0]
    tgt_count = box_weights.shape[1]
    vec_len = box_weights.shape[2]
    current = box_weights
    bit_idx = 0
    level_idx = bit_idx
    my_child = sub_index // 2**bit_idx % 2
    omegas = level_omegas(velocity, device, level_idx, tgt_count)
    own_term = own_part(current, omegas, my_child, level_idx)
    partner = swapped(current, "sub", bit_idx)
    current = far_part(own_term, partner, omegas, my_child, level_idx)
    spread = lax.all_to_all(current, "box", split_axis=1, concat_axis=0, tiled=True)
    block_width = tgt_count // box_count
    for bit_idx in range(box_bits):
        level_idx = sub_bits + bit_idx
        weights, coord_in, coord_out = level_tables(level_idx % 2)
        row_count = spread.shape[0]
        col_count = spread.shape[1]
        groups = 2 ** (bit_idx + 1)
        vel_table = velocity[: sub_count * groups * tgt_count].reshape(groups, sub_count, tgt_count)
        omegas = lax.dynamic_slice(
            vel_table, (0, sub_index, box_index * block_width), (groups, 1, block_width)
        )
        omegas = omegas.reshape(2, col_count)
        blocks = spread.reshape(row_count // (2 * src_count), 2, src_count, col_count, vec_len)
        merged = merge_blocks(blocks, omegas, weights, coord_in, coord_out)
        spread = merged.reshape(row_count // 2, 2 * col_count, vec_len)
        if level_idx == levels // 2 - 1:
            spread = apply_switch(spread, switch_kernel)
    current = lax.all_to_all(spread, "box", split_axis=1, concat_axis=1, tiled=True)
    return current


def solution(mesh):
    return jax.shard_map(
        body,
        mesh=mesh,
        in_specs=(P(("shot", "box", "sub"), None, None), P("shot"), P()),
        out_specs=P("shot", ("box", "sub"), None),
        check_vma=False,
    )
```

profile of v0, /device:TPU:0, one launch (start us, length us, event | category | flops | bytes accessed | tf_op | source)
XLA Modules:
  0.0 46.1 jit_solution(10633600639100690880)
XLA Ops:
  0.0 0.5 %collective-permute-start = (f32[2,256,128]{2,1,0:T(8,128)}, f32[2,256,128]{2,1,0:T(8,128)S(1)}, u32[]{:S(2)}, u32[]{:S(2)}) collective-permute-start(f32[2,256,128]{2,1,0:T(8,128)} %param.3), channel_id=1, source_target_pairs={{0,1},{1,0},{2,3},{3,2},{4,5},{5,4},{6,7},{7,6},{8,9},{9,8},{10,11... | collective-permute-start | bytes 786440 | tf_op jit(solution)/shard_map/ppermute | solution.py:13
  0.7 0.7 %copy-done.2 = f32[4096]{0:T(1024)S(1)} copy-done((f32[4096]{0:T(1024)S(1)}, f32[4096]{0:T(1024)}, u32[]{:S(2)}) %copy-start.2) | copy-done | bytes 16408
  2.0 0.3 select_reduce_fusion.1
  3.2 0.5 %slice-done.1 = f32[2048]{0:T(1024)S(1)} async-done(((f32[4096]{0:T(1024)}), f32[2048]{0:T(1024)S(1)}, s32[]{:S(2)}) %slice-start.1) | async-done | bytes 8216 | tf_op jit(solution)/shard_map/slice | solution.py:155
  3.9 0.3 multiply_cosine_fusion.5
  4.2 0.3 multiply_cosine_fusion.8
  4.6 0.4 slice-done
  5.2 0.3 broadcast_select_fusion
  5.9 0.5 %multiply_cosine_fusion.7 = (f32[2,64,64]{2,1,0:T(8,128)S(1)}, f32[2,64,64]{2,1,0:T(8,128)S(1)}, f32[2,64,64]{2,1,0:T(8,128)S(1)}, f32[2,64,64]{2,1,0:T(8,128)S(1)}) fusion(f32[64]{0:T(128)S(1)} %squeeze_stack_reshape.16, f32[2,64]{1,0:T(2,128)S(1)} %neg.34, f32[64]{0:T(128)S(1)} %squeeze_stack_reshape.17), kind=kLoop, calls=%fused_computation.103 | loop fusion | flops 16384 | bytes 132096 | tf_op jit(solution)/shard_map/cos | solution.py:59
  6.6 1.0 %multiply_cosine_fusion.2 = (f32[256,64]{1,0:T(8,128)S(1)}, f32[256,64]{1,0:T(8,128)S(1)}, f32[256,64]{1,0:T(8,128)S(1)}, f32[256,64]{1,0:T(8,128)S(1)}) fusion(f32[64]{0:T(128)S(1)} %get-tuple-element.97, f32[256]{0:T(256)S(1)} %get-tuple-element.7, f32[64]{0:T(128)S(1)} %get-tuple-element.98), kind=kLoop, calls=%fused_computation.59 | loop fusion | flops 32768 | bytes 263680 | tf_op jit(solution)/shard_map/cos | solution.py:59
  7.9 0.3 multiply_cosine_fusion.4
  8.2 0.3 multiply_cosine_fusion.11
  9.1 0.4 fusion.39
  9.8 0.4 convolution_add_fusion
  10.6 0.8 %copy.29 = f32[2,256,128]{2,0,1:T(2,128)} copy(f32[2,256,128]{1,2,0:T(8,128)S(1)} %maximum_multiply_fusion) | data formatting | bytes 524288 | tf_op jit(solution)/shard_map/mul | solution.py:124
  11.4 6.8 %all-to-all-start = ((f32[2,256,128]{2,0,1:T(2,128)}), f32[2,256,128]{2,0,1:T(2,128)S(1)}, u32[]{:S(2)}, u32[]{:S(2)}) async-start(f32[2,256,128]{2,0,1:T(2,128)} %copy.29), calls=%async_computation | async-start | bytes 524288 | tf_op jit(solution)/shard_map/all_to_all | solution.py:147
  18.4 1.0 %multiply_cosine_fusion.1 = (f32[2,128,64]{2,1,0:T(8,128)S(1)}, f32[2,128,64]{2,1,0:T(8,128)S(1)}, f32[2,128,64]{2,1,0:T(8,128)S(1)}, f32[2,128,64]{2,1,0:T(8,128)S(1)}) fusion(f32[64]{0:T(128)S(1)} %mul.1317, f32[2,128]{1,0:T(2,128)S(1)} %neg.35, f32[64]{0:T(128)S(1)} %mul.1330), kind=kLoop, calls=%fused_computation.57 | loop fusion | flops 32768 | bytes 263680 | tf_op jit(solution)/shard_map/cos | solution.py:59
  19.4 8.4 %all-to-all-done = f32[2,256,128]{2,0,1:T(2,128)S(1)} async-done(((f32[2,256,128]{2,0,1:T(2,128)}), f32[2,256,128]{2,0,1:T(2,128)S(1)}, u32[]{:S(2)}, u32[]{:S(2)}) %all-to-all-start) | async-done | bytes 262176 | tf_op jit(solution)/shard_map/all_to_all | solution.py:147
  28.3 0.7 %fusion = f32[4,2,2,32,128]{4,3,2,1,0:T(8,128)S(1)} fusion(f32[4,2,2,32,64]{4,3,2,1,0:T(8,128)S(1)} %get-tuple-element.32, f32[4,2,2,32,64]{4,3,2,1,0:T(8,128)S(1)} %get-tuple-element.31, f32[4,2,2,32,64]{4,3,2,1,0:T(8,128)S(1)} %get-tuple-element.30, f32[4,2,2,32,64]{4,3,2,1,0:T(8,128)S(1)} %get-tuple-element.29, ...), kind=kOutput, calls=%fused_computation.2 | convolution fusion | flops 201719808 | bytes 917504 | tf_op jit(solution)/shard_map/dot_general | solution.py:72
  29.1 0.4 fusion.22
  29.9 0.7 %fusion.8 = f32[2,2,2,64,128]{4,3,2,1,0:T(8,128)S(1)} fusion(f32[2,2,2,64,64]{4,3,2,1,0:T(8,128)S(1)} %get-tuple-element.24, f32[2,2,2,64,64]{4,3,2,1,0:T(8,128)S(1)} %get-tuple-element.23, f32[2,2,2,64,64]{4,3,2,1,0:T(8,128)S(1)} %get-tuple-element.22, f32[2,2,2,64,64]{4,3,2,1,0:T(8,128)S(1)} %get-tuple-element.21, f32[128,128]{1,0:T(8,128)S(1)} %mul.1392, ...), kind=kOutput, calls=%fused_computation.10 | convolution fusion | flops 201752576 | bytes 917504 | tf_op jit(solution)/shard_map/dot_general | solution.py:72
  31.3 0.9 %convolution_bitcast_fusion = f32[1,2,2,128,128]{3,4,2,1,0:T(8,128)S(1)} fusion(f32[1,2,2,128,64]{4,3,2,1,0:T(8,128)S(1)} %get-tuple-element.12, f32[1,2,2,128,64]{4,3,2,1,0:T(8,128)S(1)} %get-tuple-element.11, f32[1,2,2,128,64]{4,3,2,1,0:T(8,128)S(1)} %get-tuple-element.104, f32[1,2,2,128,64]{4,3,2,1,0:T(8,128)S(1)} %get-tuple-element.105, ...), kind=kOutput, calls=%fused_computation | convolution fusion | flops 201719808 | bytes 917504 | tf_op jit(solution)/shard_map/dot_general | solution.py:72
  32.8 12.5 %all_to_all.20 = f32[2,256,128]{2,0,1:T(2,128)S(1)} all-to-all(f32[2,256,128]{2,0,1:T(2,128)S(1)} %copy.35), channel_id=1, replica_groups=mesh['shot'=2,'box'=8,'sub'=2] {'box'}, dimensions={1} | all-to-all | bytes 524288 | tf_op jit(solution)/shard_map/all_to_all | solution.py:165
  45.3 0.7 %copy.36 = f32[2,256,128]{2,1,0:T(8,128)} copy(f32[2,256,128]{2,0,1:T(2,128)S(1)} %all_to_all.20) | data formatting | bytes 524288 | tf_op jit(solution)/shard_map/all_to_all | solution.py:165
  (90 shorter events, 6.4 us)
Async XLA Ops:
  0.0 29.1 %copy-start = (f32[128,128]{1,0:T(8,128)S(1)}, f32[128,128]{1,0:T(8,128)}, u32[]{:S(2)}) copy-start(f32[128,128]{1,0:T(8,128)} %param.5) | copy-start | bytes 196612
  0.0 9.4 %collective-permute-start = (f32[2,256,128]{2,1,0:T(8,128)}, f32[2,256,128]{2,1,0:T(8,128)S(1)}, u32[]{:S(2)}, u32[]{:S(2)}) collective-permute-start(f32[2,256,128]{2,1,0:T(8,128)} %param.3), channel_id=1, source_target_pairs={{0,1},{1,0},{2,3},{3,2},{4,5},{5,4},{6,7},{7,6},{8,9},{9,8},{10,11... | collective-permute-start | bytes 786440 | tf_op jit(solution)/shard_map/ppermute | solution.py:13
  0.7 0.7 %copy-start.2 = (f32[4096]{0:T(1024)S(1)}, f32[4096]{0:T(1024)}, u32[]{:S(2)}) copy-start(f32[4096]{0:T(1024)} %param.4) | copy-start | bytes 49156
  3.0 0.7 %slice-start.1 = ((f32[4096]{0:T(1024)}), f32[2048]{0:T(1024)S(1)}, s32[]{:S(2)}) async-start(f32[4096]{0:T(1024)} %param.4), calls=%async_computation.3 | async-start | bytes 16384 | tf_op jit(solution)/shard_map/slice | solution.py:155
  4.2 0.7 %slice-start = ((f32[4096]{0:T(1024)}), f32[1024]{0:T(1024)S(1)}, s32[]{:S(2)}) async-start(f32[4096]{0:T(1024)} %param.4), calls=%async_computation.2 | async-start | bytes 8192 | tf_op jit(solution)/shard_map/slice | solution.py:155
  6.6 1.0 %copy-start.1 = (f32[2,256,128]{2,1,0:T(8,128)S(1)}, f32[2,256,128]{2,1,0:T(8,128)}, u32[]{:S(2)}) copy-start(f32[2,256,128]{2,1,0:T(8,128)} %param.3) | copy-start | bytes 786436
  11.4 16.4 %all-to-all-start = ((f32[2,256,128]{2,0,1:T(2,128)}), f32[2,256,128]{2,0,1:T(2,128)S(1)}, u32[]{:S(2)}, u32[]{:S(2)}) async-start(f32[2,256,128]{2,0,1:T(2,128)} %copy.29), calls=%async_computation | async-start | bytes 524288 | tf_op jit(solution)/shard_map/all_to_all | solution.py:147
where the time goes:
time: 46.4 us; the launch traced here: 46.1 us
  blocking collectives  12.5 us (27%)
  waiting for transfers between devices  8.38 us (18%)
  starting transfers between devices  7.3 us (16%)
  local copies, waits for them, and re-layouts  7.19 us (15%)
  other arithmetic  6.78 us (15%)
  matrix products  3.37 us (7%)
  between operations  0.55 us (1%)
    all_to_all x1, blocking collectives, body(): lax.all_to_all(spread, 'box', split_axis=1, concat_axis=1, tiled=True)  12.5 us
    all_to_all x1, waiting for transfers between devices, body(): lax.all_to_all(current, 'box', split_axis=1, concat_axis=0, tiled=True)  8.38 us
    all_to_all x1, starting transfers between devices, body(): lax.all_to_all(current, 'box', split_axis=1, concat_axis=0, tiled=True)  6.81 us
    cos x8, other arithmetic, rotate(): cosines = jnp.cos(angles)  3.91 us
    dot_general x3, matrix products, merge_blocks(): jnp.dot(joined.reshape(-1, 4 * CHEB * CHEB), weights, precision=lax.Preci...  2.23 us
    sub x11, other arithmetic, rotate(): real_part * cosines - imag_part * sine_vals  1.13 us
    unnamed x9, local copies, waits for them, and re-layouts  0.93 us
    slice x6, local copies, waits for them, and re-layouts, body(): velocity[:sub_count * groups * tgt_count]  0.93 us
  transfers between devices with their start and end apart: 2, of which 1 were waited for; matrix products, arithmetic and copies ran while one was open for 18% of the time, Pallas kernels for 0%

commit v1 on v0

--- a/solution.py
+++ b/solution.py
@@ -162,7 +162,10 @@
         spread = merged.reshape(row_count // 2, 2 * col_count, vec_len)
         if level_idx == levels // 2 - 1:
             spread = apply_switch(spread, switch_kernel)
-    current = lax.all_to_all(spread, "box", split_axis=1, concat_axis=1, tiled=True)
+    current = jnp.concatenate(
+        lax.all_to_all(jnp.stack(jnp.split(spread, lax.axis_size("box"), axis=1)), "box", 0, 0),
+        axis=1,
+    )
     return current
 
 

time: 46.4 us -> 47.3 us (1.019)
  local copies, waits for them, and re-layouts: 7.19 us -> 7.95 us
    another operation x0 -> x10, local copies, waits for them, and re-layouts: none -> 0.86 us  [body(): jnp.stack(jnp.split(spread, lax.axis_size('box'), axis=1))]
    unnamed x9 -> x16, local copies, waits for them, and re-layouts: 0.93 us -> 0.98 us
where the time goes in v1:
time: 47.3 us; the launch traced here: 46.9 us
  blocking collectives  12.5 us (26%)
  waiting for transfers between devices  8.39 us (18%)
  local copies, waits for them, and re-layouts  7.95 us (17%)
  starting transfers between devices  7.3 us (15%)
  other arithmetic  6.78 us (14%)
  matrix products  3.36 us (7%)
  between operations  0.61 us (1%)
    all_to_all x1, blocking collectives, body(): lax.all_to_all(jnp.stack(jnp.split(spread, lax.axis_size('box'), axis=1))...  12.5 us
    all_to_all x1, waiting for transfers between devices, body(): lax.all_to_all(current, 'box', split_axis=1, concat_axis=0, tiled=True)  8.39 us
    all_to_all x1, starting transfers between devices, body(): lax.all_to_all(current, 'box', split_axis=1, concat_axis=0, tiled=True)  6.81 us
    cos x8, other arithmetic, rotate(): cosines = jnp.cos(angles)  3.91 us
    dot_general x3, matrix products, merge_blocks(): jnp.dot(joined.reshape(-1, 4 * CHEB * CHEB), weights, precision=lax.Preci...  2.22 us
    sub x11, other arithmetic, rotate(): real_part * cosines - imag_part * sine_vals  1.13 us
    unnamed x16, local copies, waits for them, and re-layouts  0.98 us
  transfers between devices with their start and end apart: 2, of which 1 were waited for; matrix products, arithmetic and copies ran while one was open for 18% of the time, Pallas kernels for 0%

profile of v1, /device:TPU:0, one launch (start us, length us, event | category | flops | bytes accessed | tf_op | source)
XLA Modules:
  0.0 46.9 jit_solution(17246111410913480117)
XLA Ops:
  0.0 0.5 %collective-permute-start = (f32[2,256,128]{2,1,0:T(8,128)}, f32[2,256,128]{2,1,0:T(8,128)S(1)}, u32[]{:S(2)}, u32[]{:S(2)}) collective-permute-start(f32[2,256,128]{2,1,0:T(8,128)} %param.3), channel_id=1, source_target_pairs={{0,1},{1,0},{2,3},{3,2},{4,5},{5,4},{6,7},{7,6},{8,9},{9,8},{10,11... | collective-permute-start | bytes 786440 | tf_op jit(solution)/shard_map/ppermute | solution.py:13
  0.7 0.7 %copy-done.2 = f32[4096]{0:T(1024)S(1)} copy-done((f32[4096]{0:T(1024)S(1)}, f32[4096]{0:T(1024)}, u32[]{:S(2)}) %copy-start.2) | copy-done | bytes 16408
  2.0 0.3 select_reduce_fusion.1
  3.2 0.5 %slice-done.1 = f32[2048]{0:T(1024)S(1)} async-done(((f32[4096]{0:T(1024)}), f32[2048]{0:T(1024)S(1)}, s32[]{:S(2)}) %slice-start.1) | async-done | bytes 8216 | tf_op jit(solution)/shard_map/slice | solution.py:155
  3.9 0.3 multiply_cosine_fusion.5
  4.2 0.3 multiply_cosine_fusion.8
  4.6 0.4 slice-done
  5.2 0.3 broadcast_select_fusion
  5.9 0.5 %multiply_cosine_fusion.7 = (f32[2,64,64]{2,1,0:T(8,128)S(1)}, f32[2,64,64]{2,1,0:T(8,128)S(1)}, f32[2,64,64]{2,1,0:T(8,128)S(1)}, f32[2,64,64]{2,1,0:T(8,128)S(1)}) fusion(f32[64]{0:T(128)S(1)} %squeeze_stack_reshape.16, f32[2,64]{1,0:T(2,128)S(1)} %neg.34, f32[64]{0:T(128)S(1)} %squeeze_stack_reshape.17), kind=kLoop, calls=%fused_computation.111 | loop fusion | flops 16384 | bytes 132096 | tf_op jit(solution)/shard_map/cos | solution.py:59
  6.6 1.0 %multiply_cosine_fusion.2 = (f32[256,64]{1,0:T(8,128)S(1)}, f32[256,64]{1,0:T(8,128)S(1)}, f32[256,64]{1,0:T(8,128)S(1)}, f32[256,64]{1,0:T(8,128)S(1)}) fusion(f32[64]{0:T(128)S(1)} %get-tuple-element.105, f32[256]{0:T(256)S(1)} %get-tuple-element.7, f32[64]{0:T(128)S(1)} %get-tuple-element.106), kind=kLoop, calls=%fused_computation.59 | loop fusion | flops 32768 | bytes 263680 | tf_op jit(solution)/shard_map/cos | solution.py:59
  7.9 0.3 multiply_cosine_fusion.4
  8.2 0.3 multiply_cosine_fusion.11
  9.1 0.4 fusion.39
  9.8 0.4 convolution_add_fusion
  10.6 0.8 %copy.46 = f32[2,256,128]{2,0,1:T(2,128)} copy(f32[2,256,128]{1,2,0:T(8,128)S(1)} %maximum_multiply_fusion) | data formatting | bytes 524288 | tf_op jit(solution)/shard_map/mul | solution.py:124
  11.4 6.8 %all-to-all-start = ((f32[2,256,128]{2,0,1:T(2,128)}), f32[2,256,128]{2,0,1:T(2,128)S(1)}, u32[]{:S(2)}, u32[]{:S(2)}) async-start(f32[2,256,128]{2,0,1:T(2,128)} %copy.46), calls=%async_computation | async-start | bytes 524288 | tf_op jit(solution)/shard_map/all_to_all | solution.py:147
  18.4 1.0 %multiply_cosine_fusion.1 = (f32[2,128,64]{2,1,0:T(8,128)S(1)}, f32[2,128,64]{2,1,0:T(8,128)S(1)}, f32[2,128,64]{2,1,0:T(8,128)S(1)}, f32[2,128,64]{2,1,0:T(8,128)S(1)}) fusion(f32[64]{0:T(128)S(1)} %mul.1317, f32[2,128]{1,0:T(2,128)S(1)} %neg.35, f32[64]{0:T(128)S(1)} %mul.1330), kind=kLoop, calls=%fused_computation.57 | loop fusion | flops 32768 | bytes 263680 | tf_op jit(solution)/shard_map/cos | solution.py:59
  19.4 8.4 %all-to-all-done = f32[2,256,128]{2,0,1:T(2,128)S(1)} async-done(((f32[2,256,128]{2,0,1:T(2,128)}), f32[2,256,128]{2,0,1:T(2,128)S(1)}, u32[]{:S(2)}, u32[]{:S(2)}) %all-to-all-start) | async-done | bytes 262176 | tf_op jit(solution)/shard_map/all_to_all | solution.py:147
  28.3 0.7 %fusion = f32[4,2,2,32,128]{4,3,2,1,0:T(8,128)S(1)} fusion(f32[4,2,2,32,64]{4,3,2,1,0:T(8,128)S(1)} %get-tuple-element.32, f32[4,2,2,32,64]{4,3,2,1,0:T(8,128)S(1)} %get-tuple-element.31, f32[4,2,2,32,64]{4,3,2,1,0:T(8,128)S(1)} %get-tuple-element.30, f32[4,2,2,32,64]{4,3,2,1,0:T(8,128)S(1)} %get-tuple-element.29, ...), kind=kOutput, calls=%fused_computation.2 | convolution fusion | flops 201719808 | bytes 917504 | tf_op jit(solution)/shard_map/dot_general | solution.py:72
  29.1 0.4 fusion.22
  29.9 0.7 %fusion.8 = f32[2,2,2,64,128]{4,3,2,1,0:T(8,128)S(1)} fusion(f32[2,2,2,64,64]{4,3,2,1,0:T(8,128)S(1)} %get-tuple-element.24, f32[2,2,2,64,64]{4,3,2,1,0:T(8,128)S(1)} %get-tuple-element.23, f32[2,2,2,64,64]{4,3,2,1,0:T(8,128)S(1)} %get-tuple-element.22, f32[2,2,2,64,64]{4,3,2,1,0:T(8,128)S(1)} %get-tuple-element.21, f32[128,128]{1,0:T(8,128)S(1)} %mul.1392, ...), kind=kOutput, calls=%fused_computation.10 | convolution fusion | flops 201752576 | bytes 917504 | tf_op jit(solution)/shard_map/dot_general | solution.py:72
  31.3 0.9 %convolution_bitcast_fusion = f32[1,2,2,128,128]{3,4,2,1,0:T(8,128)S(1)} fusion(f32[1,2,2,128,64]{4,3,2,1,0:T(8,128)S(1)} %get-tuple-element.12, f32[1,2,2,128,64]{4,3,2,1,0:T(8,128)S(1)} %get-tuple-element.11, f32[1,2,2,128,64]{4,3,2,1,0:T(8,128)S(1)} %get-tuple-element.112, f32[1,2,2,128,64]{4,3,2,1,0:T(8,128)S(1)} %get-tuple-element.113, ...), kind=kOutput, calls=%fused_computation | convolution fusion | flops 201719808 | bytes 917504 | tf_op jit(solution)/shard_map/dot_general | solution.py:72
  33.7 12.5 %all_to_all.20 = f32[8,2,32,128]{3,2,1,0:T(8,128)S(1)} all-to-all(f32[8,2,32,128]{3,2,1,0:T(8,128)S(1)} %constant_dynamic-update-slice_fusion.2), channel_id=1, replica_groups=mesh['shot'=2,'box'=8,'sub'=2] {'box'}, dimensions={0} | all-to-all | bytes 524288 | tf_op jit(solution)/shard_map/all_to_all | solution.py:166
  46.2 0.7 %copy.60 = f32[8,2,32,128]{3,2,0,1:T(8,128)} copy(f32[8,2,32,128]{3,2,1,0:T(8,128)S(1)} %all_to_all.20) | data formatting | bytes 524288 | tf_op jit(solution)/shard_map/all_to_all | solution.py:166
  (106 shorter events, 7.2 us)
Async XLA Ops:
  0.0 29.1 %copy-start = (f32[128,128]{1,0:T(8,128)S(1)}, f32[128,128]{1,0:T(8,128)}, u32[]{:S(2)}) copy-start(f32[128,128]{1,0:T(8,128)} %param.5) | copy-start | bytes 196612
  0.0 9.4 %collective-permute-start = (f32[2,256,128]{2,1,0:T(8,128)}, f32[2,256,128]{2,1,0:T(8,128)S(1)}, u32[]{:S(2)}, u32[]{:S(2)}) collective-permute-start(f32[2,256,128]{2,1,0:T(8,128)} %param.3), channel_id=1, source_target_pairs={{0,1},{1,0},{2,3},{3,2},{4,5},{5,4},{6,7},{7,6},{8,9},{9,8},{10,11... | collective-permute-start | bytes 786440 | tf_op jit(solution)/shard_map/ppermute | solution.py:13
  0.7 0.7 %copy-start.2 = (f32[4096]{0:T(1024)S(1)}, f32[4096]{0:T(1024)}, u32[]{:S(2)}) copy-start(f32[4096]{0:T(1024)} %param.4) | copy-start | bytes 49156
  3.0 0.7 %slice-start.1 = ((f32[4096]{0:T(1024)}), f32[2048]{0:T(1024)S(1)}, s32[]{:S(2)}) async-start(f32[4096]{0:T(1024)} %param.4), calls=%async_computation.3 | async-start | bytes 16384 | tf_op jit(solution)/shard_map/slice | solution.py:155
  4.2 0.7 %slice-start = ((f32[4096]{0:T(1024)}), f32[1024]{0:T(1024)S(1)}, s32[]{:S(2)}) async-start(f32[4096]{0:T(1024)} %param.4), calls=%async_computation.2 | async-start | bytes 8192 | tf_op jit(solution)/shard_map/slice | solution.py:155
  6.6 1.0 %copy-start.1 = (f32[2,256,128]{2,1,0:T(8,128)S(1)}, f32[2,256,128]{2,1,0:T(8,128)}, u32[]{:S(2)}) copy-start(f32[2,256,128]{2,1,0:T(8,128)} %param.3) | copy-start | bytes 786436
  11.4 16.4 %all-to-all-start = ((f32[2,256,128]{2,0,1:T(2,128)}), f32[2,256,128]{2,0,1:T(2,128)S(1)}, u32[]{:S(2)}, u32[]{:S(2)}) async-start(f32[2,256,128]{2,0,1:T(2,128)} %copy.46), calls=%async_computation | async-start | bytes 524288 | tf_op jit(solution)/shard_map/all_to_all | solution.py:147
